TPU v7x, 32 devices: a whole 2x2x4 slice. The times are simulated.
32 devices in a mesh: dp: 8 (over z, y), tensor: 4 (over x, core).
Axes of the slice: x: 2, y: 2, z: 4, core: 2. Of those that a mesh axis runs over, the one named last changes fastest.
Arguments:
- tokens: bfloat16 [12288, 768], P('dp', 'tensor'), may hold values from -6 to 6
- cotangent: bfloat16 [12288, 768], P('dp', 'tensor'), may hold values from -6 to 6
- seq_start: int32 [12288], P('dp'), may hold values from 0 to 384, as said below
- row_place: int32 [8, 1536], P('dp'), may hold values from 0 to 1535, each once within a row
- qkv_weight: bfloat16 [3, 768, 768], P(None, None, 'tensor'), may hold values from -0.21875 to 0.21875
- qv_bias: bfloat16 [2, 768], P(None, 'tensor'), may hold values from -1.5 to 1.5
- out_weight: bfloat16 [768, 768], P('tensor'), may hold values from -0.875 to 0.875
- out_bias: bfloat16 [768], replicated, may hold values from -1.5 to 1.5
- first_gain: bfloat16 [768], replicated, may hold values from 0.5 to 1.5
- first_shift: bfloat16 [768], replicated, may hold values from -1.5 to 1.5
- up_weight: bfloat16 [2, 768, 3072], P(None, None, 'tensor'), may hold values from -0.21875 to 0.21875
- up_bias: bfloat16 [2, 3072], P(None, 'tensor'), may hold values from -1.5 to 1.5
- down_weight: bfloat16 [3072, 768], P('tensor'), may hold values from -0.15625 to 0.15625
- down_bias: bfloat16 [768], replicated, may hold values from -1.5 to 1.5
- second_gain: bfloat16 [768], replicated, may hold values from 0.5 to 1.5
- second_shift: bfloat16 [768], replicated, may hold values from -1.5 to 1.5
Outputs:
- layer_out: bfloat16 [12288, 768], P('dp', 'tensor')
- input_grad: bfloat16 [12288, 768], P('dp', 'tensor')
- qkv_grad: float32 [3, 768, 768], P(None, 'dp', 'tensor')
- qv_bias_grad: float32 [2, 768], P(None, 'tensor')
- out_grad: float32 [768, 768], P('tensor', 'dp')
- out_bias_grad: float32 [768], P('dp')
- first_gain_grad: float32 [768], P('dp')
- first_shift_grad: float32 [768], P('dp')
- up_grad: float32 [2, 768, 3072], P(None, 'dp', 'tensor')
- up_bias_grad: float32 [2, 3072], P(None, 'tensor')
- down_grad: float32 [3072, 768], P('tensor', 'dp')
- down_bias_grad: float32 [768], P('dp')
- second_gain_grad: float32 [768], P('dp')
- second_shift_grad: float32 [768], P('dp')
Inputs may be any that keep to these rules, and one draw needn't show every extreme that they name: seq_start of a token is the offset, within its aligned block of 512 packed rows, of the first token of its sequence; sequences are 128, 256 or 512 tokens long, begin at multiples of 128 and never cross a block. Each row of row_place is a permutation of 0 to 1535.
All inputs are finite; a program needn't handle non-finite values.
Results may differ from a plain program's by a relative error of at most 0.02.
The roundings to bfloat16 on the way count: a program that leaves them out, or rounds other values in their place, can miss the bound.
Values may be sent and summed in bfloat16 or wider, within the bound.
A program may use at most 128 MiB of HBM per device.

v0:
```python
import jax
import jax.numpy as jnp
from jax import lax
from jax.sharding import PartitionSpec as P

HEADS = 12
HEAD_DIM = 64
BLOCK = 512


def layer_norm(values, scale_row, shift_row):
    center = values - jnp.mean(values, axis=-1, keepdims=True)
    spread = jnp.mean(center * center, axis=-1, keepdims=True)
    return center * lax.rsqrt(spread + 1e-05) * scale_row + shift_row


def gated_unit(gate_part, value_part):
    return jax.nn.gelu(gate_part, approximate=False) * value_part


def alibi_terms(part_index, local_heads, block_rows):
    heads_idx = (part_index * local_heads + jnp.arange(local_heads)).astype(jnp.float32)
    slopes = 2.0 ** (-8.0 * (heads_idx + 1.0) / HEADS)
    position = jnp.arange(block_rows).astype(jnp.float32)
    distance = jnp.abs(position[:, None] - position[None, :])
    return -slopes[:, None, None] * distance[None]


def block_scores(queries, key_rows, alibi_bias, same_seq, score_scale):
    raw_scores = jnp.einsum(
        "bqhe,bkhe->bhqk", queries, key_rows, preferred_element_type=jnp.float32
    )
    scored = raw_scores * score_scale + alibi_bias[None]
    return jnp.where(same_seq[:, None], scored, -1e30)


def softmax_rows(scored):
    row_max = jnp.max(scored, axis=-1, keepdims=True)
    exponent = jnp.exp(scored - row_max)
    denominator = jnp.sum(exponent, axis=-1, keepdims=True)
    return (exponent / denominator, row_max + jnp.log(denominator))


def on_device(
    tokens,
    cotangent,
    seq_start,
    row_place,
    qkv_weight,
    qv_bias,
    out_weight,
    out_bias,
    first_gain,
    first_shift,
    up_weight,
    up_bias,
    down_weight,
    down_bias,
    second_gain,
    second_shift,
):
    arr_tokens, arr_cot = (
        lax.all_to_all(tokens, "dp", split_axis=0, concat_axis=0, tiled=True),
        lax.all_to_all(cotangent, "dp", split_axis=0, concat_axis=0, tiled=True),
    )
    wide_tokens, wide_cot = (
        lax.all_gather(arr_tokens, "tensor", axis=1, tiled=True),
        lax.all_gather(arr_cot, "tensor", axis=1, tiled=True),
    )
    slot_index = row_place[0]
    packed_in = jnp.zeros_like(wide_tokens).at[slot_index].set(wide_tokens)
    packed_cot = jnp.zeros_like(wide_cot).at[slot_index].set(wide_cot)
    row_count = packed_in.shape[0]
    columns = packed_in.shape[1]
    local_heads = qkv_weight.shape[2] // HEAD_DIM
    block_rows = BLOCK
    blocks = row_count // block_rows
    part_index = lax.axis_index("tensor")
    col_count = columns // lax.axis_size("tensor")
    score_scale = HEAD_DIM ** (-0.5)
    alibi_bias = alibi_terms(part_index, local_heads, block_rows)
    block_starts = seq_start.reshape(blocks, block_rows)
    same_seq = block_starts[:, :, None] == block_starts[:, None, :]
    bias_rows = jnp.stack([qv_bias[0], jnp.zeros_like(qv_bias[0]), qv_bias[1]]).astype(jnp.float32)
    projected = jnp.einsum("td,kde->kte", packed_in, qkv_weight, preferred_element_type=jnp.float32)
    qkv_rows = (projected + bias_rows[:, None, :]).astype(jnp.bfloat16)
    split_heads = qkv_rows.reshape(3, blocks, block_rows, local_heads, HEAD_DIM)
    queries = split_heads[0]
    key_rows = split_heads[1]
    value_rows = split_heads[2]
    attn_probs, log_total = softmax_rows(
        block_scores(queries, key_rows, alibi_bias, same_seq, score_scale)
    )
    context = jnp.einsum(
        "bhqk,bkhe->bqhe",
        attn_probs.astype(jnp.bfloat16),
        value_rows,
        preferred_element_type=jnp.float32,
    )
    context = context.reshape(row_count, local_heads * HEAD_DIM).astype(jnp.bfloat16)
    attn_part = jnp.dot(context, out_weight, preferred_element_type=jnp.float32)
    attended = lax.psum(attn_part, "tensor")
    hidden = packed_in.astype(jnp.float32) + (attended + out_bias.astype(jnp.float32))
    normed, first_pull = jax.vjp(
        layer_norm, hidden, first_gain.astype(jnp.float32), first_shift.astype(jnp.float32)
    )
    normed_low = normed.astype(jnp.bfloat16)
    lifted = jnp.einsum("td,kdf->ktf", normed_low, up_weight, preferred_element_type=jnp.float32)
    lifted = lifted + up_bias.astype(jnp.float32)[:, None, :]
    gated_val, gate_pull = jax.vjp(gated_unit, lifted[0], lifted[1])
    gated_low = gated_val.astype(jnp.bfloat16)
    ffn_part = jnp.dot(gated_low, down_weight, preferred_element_type=jnp.float32)
    ffn_out = lax.psum(ffn_part.astype(jnp.bfloat16), "tensor").astype(jnp.float32)
    mixed_rows = normed + (ffn_out + down_bias.astype(jnp.float32))
    result, second_pull = jax.vjp(
        layer_norm, mixed_rows, second_gain.astype(jnp.float32), second_shift.astype(jnp.float32)
    )
    grad_scale = (row_count * lax.axis_size("dp")) ** (-0.5)
    d_mixed, d_second_gain, d_second_shift = second_pull(packed_cot.astype(jnp.float32))
    d_mixed_low = d_mixed.astype(jnp.bfloat16)
    g_down = jnp.einsum("tf,td->fd", gated_low, d_mixed_low, preferred_element_type=jnp.float32)
    g_down_bias = jnp.sum(d_mixed, axis=0)
    d_gated = jnp.einsum("td,fd->tf", d_mixed_low, down_weight, preferred_element_type=jnp.float32)
    d_gate, d_value = gate_pull(d_gated)
    d_lifted = jnp.stack([d_gate, d_value]).astype(jnp.bfloat16)
    g_up = jnp.einsum("td,ktf->kdf", normed_low, d_lifted, preferred_element_type=jnp.float32)
    g_up_bias = jnp.sum(d_lifted, axis=1, dtype=jnp.float32)
    d_normed_part = jnp.einsum(
        "ktf,kdf->td", d_lifted, up_weight, preferred_element_type=jnp.float32
    )
    d_normed = d_mixed + lax.psum(d_normed_part.astype(jnp.bfloat16), "tensor").astype(jnp.float32)
    d_hidden, d_first_gain, d_first_shift = first_pull(d_normed)
    d_hidden_low = d_hidden.astype(jnp.bfloat16)
    g_out = jnp.einsum("te,td->ed", context, d_hidden_low, preferred_element_type=jnp.float32)
    g_out_bias = jnp.sum(d_hidden, axis=0)
    d_context = jnp.einsum(
        "td,ed->te", d_hidden_low, out_weight, preferred_element_type=jnp.float32
    )
    d_context = d_context.astype(jnp.bfloat16).reshape(blocks, block_rows, local_heads, HEAD_DIM)
    probs_back = jnp.exp(
        block_scores(queries, key_rows, alibi_bias, same_seq, score_scale) - log_total
    )
    d_probs = jnp.einsum(
        "bqhe,bkhe->bhqk", d_context, value_rows, preferred_element_type=jnp.float32
    )
    g_values = jnp.einsum(
        "bhqk,bqhe->bkhe",
        probs_back.astype(jnp.bfloat16),
        d_context,
        preferred_element_type=jnp.float32,
    )
    center_term = jnp.sum(probs_back * d_probs, axis=-1, keepdims=True)
    d_scores = (probs_back * (d_probs - center_term)).astype(jnp.bfloat16)
    g_queries = (
        jnp.einsum("bhqk,bkhe->bqhe", d_scores, key_rows, preferred_element_type=jnp.float32)
        * score_scale
    )
    g_keys = (
        jnp.einsum("bhqk,bqhe->bkhe", d_scores, queries, preferred_element_type=jnp.float32)
        * score_scale
    )
    d_qkv = jnp.stack([g_queries, g_keys, g_values]).reshape(3, row_count, local_heads * HEAD_DIM)
    d_qkv = d_qkv.astype(jnp.bfloat16)
    g_qkv = jnp.einsum("td,kte->kde", packed_in, d_qkv, preferred_element_type=jnp.float32)
    g_qv_bias = jnp.sum(jnp.stack([d_qkv[0], d_qkv[2]]), axis=1, dtype=jnp.float32)
    d_input_part = jnp.einsum("kte,kde->td", d_qkv, qkv_weight, preferred_element_type=jnp.float32)
    hidden_cols = lax.dynamic_slice_in_dim(d_hidden, part_index * col_count, col_count, 1)
    grad_cols = hidden_cols + lax.psum_scatter(
        d_input_part.astype(jnp.bfloat16), "tensor", scatter_dimension=1, tiled=True
    ).astype(jnp.float32)
    summed = (
        lax.psum_scatter(g_qkv * grad_scale, "dp", scatter_dimension=1, tiled=True),
        lax.psum_scatter(g_out * grad_scale, "dp", scatter_dimension=1, tiled=True),
        lax.psum_scatter(g_out_bias * grad_scale, "dp", scatter_dimension=0, tiled=True),
        lax.psum_scatter(d_first_gain * grad_scale, "dp", scatter_dimension=0, tiled=True),
        lax.psum_scatter(d_first_shift * grad_scale, "dp", scatter_dimension=0, tiled=True),
        lax.psum_scatter(g_up * grad_scale, "dp", scatter_dimension=1, tiled=True),
        lax.psum_scatter(g_down * grad_scale, "dp", scatter_dimension=1, tiled=True),
        lax.psum_scatter(g_down_bias * grad_scale, "dp", scatter_dimension=0, tiled=True),
        lax.psum_scatter(d_second_gain * grad_scale, "dp", scatter_dimension=0, tiled=True),
        lax.psum_scatter(d_second_shift * grad_scale, "dp", scatter_dimension=0, tiled=True),
    )
    qkv_grad, out_grad, out_bias_grad, first_gain_grad, first_shift_grad = (
        summed[0],
        summed[1],
        summed[2],
        summed[3],
        summed[4],
    )
    up_grad, down_grad, down_bias_grad, second_gain_grad, second_shift_grad = (
        summed[5],
        summed[6],
        summed[7],
        summed[8],
        summed[9],
    )
    qv_bias_grad, up_bias_grad = lax.psum((g_qv_bias * grad_scale, g_up_bias * grad_scale), "dp")
    layer_cols = lax.dynamic_slice_in_dim(result, part_index * col_count, col_count, 1)
    layer_back = layer_cols[slot_index].astype(jnp.bfloat16)
    grad_back = grad_cols[slot_index].astype(jnp.bfloat16)
    layer_out, input_grad = (
        lax.all_to_all(layer_back, "dp", split_axis=0, concat_axis=0, tiled=True),
        lax.all_to_all(grad_back, "dp", split_axis=0, concat_axis=0, tiled=True),
    )
    return (
        layer_out,
        input_grad,
        qkv_grad,
        qv_bias_grad,
        out_grad,
        out_bias_grad,
        first_gain_grad,
        first_shift_grad,
        up_grad,
        up_bias_grad,
        down_grad,
        down_bias_grad,
        second_gain_grad,
        second_shift_grad,
    )


def solution(mesh):
    return jax.shard_map(
        on_device,
        mesh=mesh,
        in_specs=(
            P("dp", "tensor"),
            P("dp", "tensor"),
            P("dp"),
            P("dp", None),
            P(None, None, "tensor"),
            P(None, "tensor"),
            P("tensor", None),
            P(),
            P(),
            P(),
            P(None, None, "tensor"),
            P(None, "tensor"),
            P("tensor", None),
            P(),
            P(),
            P(),
        ),
        out_specs=(
            P("dp", "tensor"),
            P("dp", "tensor"),
            P(None, "dp", "tensor"),
            P(None, "tensor"),
            P("tensor", "dp"),
            P("dp"),
            P("dp"),
            P("dp"),
            P(None, "dp", "tensor"),
            P(None, "tensor"),
            P("tensor", "dp"),
            P("dp"),
            P("dp"),
            P("dp"),
        ),
        check_vma=False,
    )
```

profile of v0, /device:TPU:0, one launch (start us, length us, event | category | flops | bytes accessed | tf_op | source)
XLA Modules:
  0.0 849.5 jit_solution(2268085062084630268)
XLA Ops:
  7.3 1.9 all_to_all.28
  9.3 27.3 %all_to_all.42 = bf16[8,192,192]{1,2,0:T(8,128)(2,1)S(1)} all-to-all(bf16[8,192,192]{1,2,0:T(8,128)(2,1)S(1)} %copy.124), channel_id=1, replica_groups=mesh['dp'=8,'tensor'=4] {'dp'}, dimensions={0} | all-to-all | bytes 1179648 | tf_op jit(solution)/shard_map/all_to_all | solution.py:63
  37.0 1.5 all_to_all.30
  40.4 2.1 broadcast_multiply_fusion
  42.5 19.2 %all-gather.3.cloned.1.call-done = bf16[1536,768]{0,1:T(8,128)(2,1)} async-done(((bf16[1536,192]{0,1:T(8,128)(2,1)}), bf16[1536,768]{0,1:T(8,128)(2,1)}) %all-gather.3.cloned.1.call-update) | async-done | bytes 2359312 | tf_op jit(solution)/shard_map/all_gather | solution.py:67
  61.7 4.3 copy.126
  66.0 10.1 %scatter_custom_fusion = bf16[1536,768]{1,0:T(8,128)(2,1)} fusion(s32[1536]{0:T(1024)S(1)} %fusion.70, bf16[1536,768]{1,0:T(8,128)(2,1)} %copy.126, bf16[]{:T(256)} %constant.46.clone.1), kind=kCustom, calls=%fused_computation.108 | custom fusion | bytes 2359808 | tf_op jit(solution)/shard_map/scatter | solution.py:71
  76.1 3.2 fusion.86
  84.3 5.3 fusion.85
  91.0 2.4 copy-done.2
  93.3 1.9 fusion.47
  95.9 2.9 fusion.87
  98.9 2.4 all_to_all.33
  101.3 2.2 copy.133
  103.5 5.5 all-to-all-start.2
  109.2 20.5 %all-to-all-done.2 = bf16[8,192,192]{1,2,0:T(8,128)(2,1)} async-done(((bf16[8,192,192]{1,2,0:T(8,128)(2,1)}), bf16[8,192,192]{1,2,0:T(8,128)(2,1)}, u32[]{:S(2)}, u32[]{:S(2)}) %all-to-all-start.2) | async-done | bytes 589856 | tf_op jit(solution)/shard_map/all_to_all | solution.py:64
  129.7 2.5 copy.134
  132.2 2.5 all_to_all.35
  134.9 58.2 %all-reduce.13.cloned.1.call-done = f32[1536,768]{1,0:T(8,128)} async-done(((f32[1536,768]{1,0:T(8,128)}), f32[1536,768]{1,0:T(8,128)}) %all-reduce.13.cloned.1.call-update) | async-done | bytes 4718608 | tf_op jit(solution)/shard_map/psum | solution.py:102
  193.1 3.8 fusion.82
  197.6 4.3 add_bitcast_fusion
  201.9 11.5 %multiply_convert_fusion.2 = (bf16[1536,768]{1,0:T(8,128)(2,1)S(1)}, f32[1536,768]{1,0:T(8,128)}) fusion(f32[2,1536,768]{2,1,0:T(8,128)S(1)} %add_bitcast_fusion), kind=kLoop, calls=%fused_computation.51 | loop fusion | flops 77856768 | bytes 16515072 | tf_op jit(solution)/shard_map/convert_element_type | solution.py:111
  214.9 3.5 convolution_convert_fusion
  219.5 4.3 copy.135
  223.7 9.8 %scatter_custom_fusion.1 = bf16[1536,768]{1,0:T(8,128)(2,1)} fusion(s32[1536]{0:T(1024)} %copy-done.29, bf16[1536,768]{1,0:T(8,128)(2,1)} %copy.135, bf16[]{:T(256)} %constant.46.clone.1), kind=kCustom, calls=%fused_computation.106 | custom fusion | bytes 2359808 | tf_op jit(solution)/shard_map/scatter | solution.py:72
  233.6 43.8 %all-reduce.15.cloned.1.call-done = bf16[1536,768]{1,0:T(8,128)(2,1)} async-done(((bf16[1536,768]{1,0:T(8,128)(2,1)}), bf16[1536,768]{1,0:T(8,128)(2,1)}) %all-reduce.15.cloned.1.call-update) | async-done | bytes 2359312 | tf_op jit(solution)/shard_map/psum | solution.py:113
  277.4 4.2 fusion.80
  281.7 2.7 fusion.4
  284.4 4.7 fusion.79
  289.2 7.1 fusion.36
  297.7 7.0 bitcast_convert_fusion.1
  305.8 54.8 %all-reduce.17.cloned.1.call-done = bf16[1536,768]{1,0:T(8,128)(2,1)} async-done(((bf16[1536,768]{1,0:T(8,128)(2,1)}), bf16[1536,768]{1,0:T(8,128)(2,1)}) %all-reduce.17.cloned.1.call-update) | async-done | bytes 2359312 | tf_op jit(solution)/shard_map/psum | solution.py:131
  360.6 6.5 multiply_reduce_fusion.1
  367.1 5.0 fusion.78
  373.2 2.2 copy-done.4
  376.9 5.3 fusion.48
  382.2 7.2 multiply_reduce_fusion
  389.4 11.2 %multiply_convert_fusion = bf16[3,3,512,512]{2,3,1,0:T(8,128)(2,1)} fusion(f32[3,3,512,512]{2,3,1,0:T(8,128)} %get-tuple-element.127, f32[3,3,512,512]{2,3,1,0:T(8,128)} %copy-done.2, f32[3,3,512]{2,1,0:T(4,128)S(1)} %get-tuple-element.126, f32[3,3,512]{2,1,0:T(4,128)S(1)} %copy-done.23), kind=kLoop, calls=%fused_computation.5 | loop fusion | flops 9437184 | bytes 23629824 | tf_op jit(solution)/shard_map/convert_element_type | solution.py:153
  400.6 4.0 fusion.51
  404.6 1.7 fusion.52
  407.9 2.7 copy.140
  410.6 1.8 stack.34
  413.8 1.8 stack.35
  417.0 4.6 fusion.31
  421.7 3.1 convolution_multiply_fusion.3
  426.1 4.5 multiply_bitcast_fusion.1
  430.6 4.2 copy.162
  434.9 4.8 reshape.283
  439.8 9.6 %multiply_bitcast_fusion = f32[2,768,768]{1,2,0:T(8,128)} fusion(bf16[1,1536,768]{2,1,0:T(8,128)(2,1)} %get-tuple-element.114, bf16[1,1536,768]{2,1,0:T(8,128)(2,1)S(1)} %copy-done.19, f32[1536,768]{1,0:T(8,128)} %copy-done.3, f32[768]{0:T(1024)S(1)} %copy-done.34, f32[768]{0:T(1024)S(1)} %copy-done.28, f32[1536]{0:T(1024)S(1)} %fusion.68, ...), kind=kOutput, calls=%fused_computation.43 | convolution fusion | flops 3633315840 | bytes 14174208 | tf_op jit(solution)/shard_map/td,ktf->kdf/dot_general | solution.py:126
  449.4 8.3 copy.150
  459.3 6.0 convolution_multiply_fusion
  465.5 2.2 fusion.38
  467.7 5.4 gather_fusion
  473.0 5.3 all-to-all-start.1
  479.6 3.1 convert_reduce_fusion
  482.7 17.3 %all-to-all-done.1 = bf16[8,192,192]{2,1,0:T(8,128)(2,1)S(1)} async-done(((bf16[8,192,192]{2,1,0:T(8,128)(2,1)}), bf16[8,192,192]{2,1,0:T(8,128)(2,1)S(1)}, u32[]{:S(2)}, u32[]{:S(2)}) %all-to-all-start.1) | async-done | bytes 589856 | tf_op jit(solution)/shard_map/all_to_all | solution.py:202
  502.4 2.2 convert_add_fusion.1
  504.7 5.4 gather_fusion.1
  510.0 3.7 all-to-all-start.3
  515.3 44.6 %all-reduce.7 = (f32[2,192]{1,0:T(2,128)}, f32[768]{0:T(1024)S(1)}, f32[768]{0:T(1024)S(1)}, f32[768]{0:T(1024)S(1)}, f32[2,768]{1,0:T(2,128)}, /*index=5*/f32[7...) all-reduce(f32[2,192]{1,0:T(2,128)S(1)} %broadcast_multiply_fusion.10, ...), channel_id=1, replica_groups=mesh['dp'=8,'tensor'=4] {'dp'}, use_global_device_ids=true, to_apply=%region_19.20 | all-reduce | flops 6528 | bytes 52224 | tf_op jit(solution)/shard_map/psum | solution.py:197
  563.4 1.6 copy.165
  565.0 32.5 %reduce-scatter.15.cloned.1.call-done = f32[96,576]{1,0:T(8,128)} async-done(((f32[768,576]{1,0:T(8,128)}), f32[96,576]{1,0:T(8,128)}) %reduce-scatter.15.cloned.1.call-update) | async-done | bytes 221200
  599.4 170.4 %all-reduce.19.cloned.1.call-done = f32[2,768,768]{2,0,1:T(2,128)} async-done(((f32[2,768,768]{2,0,1:T(2,128)}), f32[2,768,768]{2,0,1:T(2,128)}) %all-reduce.19.cloned.1.call-update) | async-done | bytes 4718608
  772.8 69.6 %reduce-scatter.11.cloned.1.call-done = f32[768,96]{0,1:T(8,128)} async-done(((f32[768,768]{0,1:T(8,128)}), f32[768,96]{0,1:T(8,128)}) %reduce-scatter.11.cloned.1.call-update) | async-done | bytes 294928 | tf_op jit(solution)/shard_map/reduce_scatter | solution.py:178
  (208 shorter events, 38.3 us)
Async XLA Ops:
  7.2 190.4 %copy-start = (bf16[2,768,768]{2,1,0:T(8,128)(2,1)S(1)}, bf16[2,768,768]{2,1,0:T(8,128)(2,1)}, u32[]{:S(2)}) copy-start(bf16[2,768,768]{2,1,0:T(8,128)(2,1)} %param.26) | copy-start | bytes 7077892
  7.2 31.4 %copy-start.39 = (s32[1536]{0:T(1024)S(1)}, s32[1536]{0:T(1024)}, u32[]{:S(2)}) copy-start(s32[1536]{0:T(1024)} %param.18) | copy-start | bytes 18436
  7.2 31.5 %copy-start.40 = (s32[1,1536]{1,0:T(1,128)S(1)}, s32[1,1536]{1,0:T(1,128)}, u32[]{:S(2)}) copy-start(s32[1,1536]{1,0:T(1,128)} %param.19) | copy-start | bytes 18436
  7.2 31.5 %copy-start.43 = (bf16[2,192]{1,0:T(2,128)(2,1)S(1)}, bf16[2,192]{1,0:T(2,128)(2,1)}, u32[]{:S(2)}) copy-start(bf16[2,192]{1,0:T(2,128)(2,1)} %param.21) | copy-start | bytes 2308
  7.2 54.5 %all-gather.3.cloned.1.call-start = ((), (), s32[]{:S(2)}) async-start(), calls=%async_computation.8 | async-start | bytes 2949120 | tf_op jit(solution)/shard_map/all_gather | solution.py:67
  38.5 154.5 %all-reduce.13.cloned.1.call-start = ((), (), s32[]{:S(2)}) async-start(), calls=%async_computation.9 | async-start | bytes 9437184 | tf_op jit(solution)/shard_map/psum | solution.py:102
  38.8 27.3 %copy-start.29 = (s32[1536]{0:T(1024)}, s32[1536]{0:T(1024)S(1)}, u32[]{:S(2)}) copy-start(s32[1536]{0:T(1024)S(1)} %fusion.70) | copy-start | bytes 18436
  40.4 35.7 %copy-start.51 = (bf16[3,768,192]{1,2,0:T(8,128)(2,1)S(1)}, bf16[3,768,192]{1,2,0:T(8,128)(2,1)}, u32[]{:S(2)}) copy-start(bf16[3,768,192]{1,2,0:T(8,128)(2,1)} %param.20) | copy-start | bytes 2654212
  84.3 5.3 copy-start.11
  89.6 3.7 copy-start.2
  89.6 3.7 copy-start.16
  98.9 10.2 %copy-start.45 = (bf16[768]{0:T(1024)(128)(2,1)S(1)}, bf16[768]{0:T(1024)(128)(2,1)}, u32[]{:S(2)}) copy-start(bf16[768]{0:T(1024)(128)(2,1)} %param.24) | copy-start | bytes 4612
  98.9 10.2 %copy-start.46 = (bf16[768]{0:T(1024)(128)(2,1)S(1)}, bf16[768]{0:T(1024)(128)(2,1)}, u32[]{:S(2)}) copy-start(bf16[768]{0:T(1024)(128)(2,1)} %param.25) | copy-start | bytes 4612
  98.9 10.3 %copy-start.47 = (bf16[768]{0:T(1024)(128)(2,1)S(1)}, bf16[768]{0:T(1024)(128)(2,1)}, u32[]{:S(2)}) copy-start(bf16[768]{0:T(1024)(128)(2,1)} %param.23) | copy-start | bytes 4612
  98.9 10.3 %copy-start.44 = (bf16[2,768]{1,0:T(2,128)(2,1)S(1)}, bf16[2,768]{1,0:T(2,128)(2,1)}, u32[]{:S(2)}) copy-start(bf16[2,768]{1,0:T(2,128)(2,1)} %param.27) | copy-start | bytes 9220
  103.5 26.2 %all-to-all-start.2 = ((bf16[8,192,192]{1,2,0:T(8,128)(2,1)}), bf16[8,192,192]{1,2,0:T(8,128)(2,1)}, u32[]{:S(2)}, u32[]{:S(2)}) async-start(bf16[8,192,192]{1,2,0:T(8,128)(2,1)} %copy.133), calls=%async_computation.2 | async-start | bytes 1572864 | tf_op jit(solution)/shard_map/all_to_all | solution.py:64
  109.1 110.4 %all-gather.5.cloned.1.call-start = ((), (), s32[]{:S(2)}) async-start(), calls=%async_computation.11 | async-start | bytes 2949120 | tf_op jit(solution)/shard_map/all_gather | solution.py:68
  109.1 258.0 %copy-start.27 = (f32[768]{0:T(1024)}, f32[768]{0:T(1024)S(1)}, u32[]{:S(2)}) copy-start(f32[768]{0:T(1024)S(1)} %convert_element_type.142) | copy-start | bytes 9220
  109.2 168.2 %copy-start.33 = (f32[768]{0:T(1024)}, f32[768]{0:T(1024)S(1)}, u32[]{:S(2)}) copy-start(f32[768]{0:T(1024)S(1)} %convert_element_type.143) | copy-start | bytes 9220
  134.7 142.7 %all-reduce.15.cloned.1.call-start = ((), (), s32[]{:S(2)}) async-start(), calls=%async_computation.10 | async-start | bytes 4718592 | tf_op jit(solution)/shard_map/psum | solution.py:113
  196.9 5.0 copy-start.3
  201.9 11.5 %copy-start.8 = (f32[2,1536,768]{2,1,0:T(8,128)}, f32[2,1536,768]{2,1,0:T(8,128)S(1)}, u32[]{:S(2)}) copy-start(f32[2,1536,768]{2,1,0:T(8,128)S(1)} %add_bitcast_fusion) | copy-start | bytes 28311556
  201.9 13.0 %copy-start.50 = (bf16[768,768]{1,0:T(8,128)(2,1)S(1)}, bf16[768,768]{1,0:T(8,128)(2,1)}, u32[]{:S(2)}) copy-start(bf16[768,768]{1,0:T(8,128)(2,1)} %param.28) | copy-start | bytes 3538948
  214.9 3.6 copy-start.41
  214.9 3.6 copy-start.48
  218.4 142.2 %all-reduce.17.cloned.1.call-start = ((), (), s32[]{:S(2)}) async-start(), calls=%async_computation.12 | async-start | bytes 4718592 | tf_op jit(solution)/shard_map/psum | solution.py:131
  277.4 4.3 copy-start.7
  281.6 7.5 slice-start
  281.7 7.5 slice-start.3
  284.4 4.7 slice-start.1
  284.4 4.7 slice-start.2
  284.4 4.7 slice-start.4
  289.1 7.2 copy-start.6
  289.1 78.0 %copy-start.25 = (f32[1536]{0:T(1024)}, f32[1536]{0:T(1024)S(1)}, u32[]{:S(2)}) copy-start(f32[1536]{0:T(1024)S(1)} %negate_multiply_fusion.2) | copy-start | bytes 18436
  304.7 196.4 %reduce-scatter.13.cloned.1.call-start = ((), (), s32[]{:S(2)}) async-start(), calls=%async_computation.14 | async-start | bytes 2949120
  360.6 6.5 copy-start.10
  373.2 3.6 copy-start.23
  376.9 5.3 copy-start.17
  389.4 11.2 %copy-start.12 = (bf16[3,512,3,64]{1,0,3,2:T(4,128)(2,1)S(1)}, bf16[3,512,3,64]{1,0,3,2:T(4,128)(2,1)}, u32[]{:S(2)}) copy-start(bf16[3,512,3,64]{1,0,3,2:T(4,128)(2,1)} %copy-done.11) | copy-start | bytes 1769476
  400.6 4.0 copy-start.5
  400.6 4.0 copy-start.15
  407.9 13.8 %copy-start.13 = (bf16[1,1536,192]{1,2,0:T(8,128)(2,1)}, bf16[1,1536,192]{1,2,0:T(8,128)(2,1)S(1)}, u32[]{:S(2)}) copy-start(bf16[1,1536,192]{1,2,0:T(8,128)(2,1)S(1)} %stack.36) | copy-start | bytes 1769476
  412.4 9.3 %copy-start.14 = (bf16[1,1536,192]{1,2,0:T(8,128)(2,1)}, bf16[1,1536,192]{1,2,0:T(8,128)(2,1)S(1)}, u32[]{:S(2)}) copy-start(bf16[1,1536,192]{1,2,0:T(8,128)(2,1)S(1)} %stack.34) | copy-start | bytes 1769476
  421.7 4.4 copy-start.9
  421.7 141.7 %reduce-scatter.17.cloned.1.call-start = ((), (), s32[]{:S(2)}) async-start(), calls=%async_computation.16 | async-start | bytes 884736
  426.0 171.4 %reduce-scatter.15.cloned.1.call-start = ((), (), s32[]{:S(2)}) async-start(), calls=%async_computation.15 | async-start | bytes 2211840
  434.9 4.9 copy-start.19
  434.9 4.9 copy-start.28
  434.9 4.9 copy-start.34
  439.7 330.1 %all-reduce.19.cloned.1.call-start = ((), (), s32[]{:S(2)}) async-start(), calls=%async_computation.17 | async-start | bytes 9437184
  457.7 7.6 copy-start.42
  457.7 7.7 copy-start.49
  457.7 7.8 copy-start.30
  457.7 384.7 %reduce-scatter.11.cloned.1.call-start = ((), (), s32[]{:S(2)}) async-start(), calls=%async_computation.13 | async-start | bytes 2654208 | tf_op jit(solution)/shard_map/reduce_scatter | solution.py:178
  467.7 10.7 %copy-start.52 = (u32[32]{0:T(128)S(1)}, u32[32]{0:T(128)}, u32[]{:S(2)}) copy-start(u32[32]{0:T(128)} %constant.120) | copy-start | bytes 388
  467.7 11.9 %copy-start.35 = (f32[768]{0:T(1024)S(1)}, f32[768]{0:T(1024)}, u32[]{:S(2)}) copy-start(f32[768]{0:T(1024)} %get-tuple-element.115) | copy-start | bytes 9220
  473.0 27.0 %all-to-all-start.1 = ((bf16[8,192,192]{2,1,0:T(8,128)(2,1)}), bf16[8,192,192]{2,1,0:T(8,128)(2,1)S(1)}, u32[]{:S(2)}, u32[]{:S(2)}) async-start(bf16[8,192,192]{2,1,0:T(8,128)(2,1)} %bitcast.11), calls=%async_computation.1 | async-start | bytes 1572864 | tf_op jit(solution)/shard_map/all_to_all | solution.py:202
  504.6 10.6 %copy-start.31 = (f32[768]{0:T(1024)S(1)}, f32[768]{0:T(1024)}, u32[]{:S(2)}) copy-start(f32[768]{0:T(1024)} %get-tuple-element.101) | copy-start | bytes 9220
  504.6 10.6 %copy-start.32 = (f32[768]{0:T(1024)S(1)}, f32[768]{0:T(1024)}, u32[]{:S(2)}) copy-start(f32[768]{0:T(1024)} %get-tuple-element.90) | copy-start | bytes 9220
  504.6 10.6 %copy-start.38 = (f32[768]{0:T(1024)S(1)}, f32[768]{0:T(1024)}, u32[]{:S(2)}) copy-start(f32[768]{0:T(1024)} %get-tuple-element.84) | copy-start | bytes 9220
  504.6 10.6 %copy-start.36 = (f32[768]{0:T(1024)S(1)}, f32[768]{0:T(1024)}, u32[]{:S(2)}) copy-start(f32[768]{0:T(1024)} %get-tuple-element.86) | copy-start | bytes 9220
  504.7 10.6 %copy-start.37 = (f32[768]{0:T(1024)S(1)}, f32[768]{0:T(1024)}, u32[]{:S(2)}) copy-start(f32[768]{0:T(1024)} %get-tuple-element.87) | copy-start | bytes 9220
  504.7 337.7 %copy-start.1 = (bf16[2,768,768]{2,1,0:T(8,128)(2,1)S(1)}, bf16[2,768,768]{2,1,0:T(8,128)(2,1)}, u32[]{:S(2)}) copy-start(bf16[2,768,768]{2,1,0:T(8,128)(2,1)} %param.26) | copy-start | bytes 7077892
  510.0 261.7 %all-to-all-start.3 = ((bf16[8,192,192]{2,1,0:T(8,128)(2,1)}), bf16[8,192,192]{2,1,0:T(8,128)(2,1)S(1)}, u32[]{:S(2)}, u32[]{:S(2)}) async-start(bf16[8,192,192]{2,1,0:T(8,128)(2,1)} %bitcast.200), calls=%async_computation.3 | async-start | bytes 1572864 | tf_op jit(solution)/shard_map/all_to_all | solution.py:203
  (7 other events, 12.3 us)
Sparse Core Ops, SparseCore 0:
  38.7 23.0 all-gather.2
  99.0 94.0 all-reduce.12
  195.2 24.1 all-gather.4
  221.7 55.6 all-reduce.14
  304.8 55.7 all-reduce.16
  421.8 32.8 reduce-scatter.12
  458.0 66.9 reduce-scatter.16
  528.5 68.9 reduce-scatter.14
  601.1 168.6 all-reduce.18
  773.7 68.6 reduce-scatter.10
where the time goes:
time: 856 us; the launch traced here: 849 us
  waiting for transfers between devices  487 us (57%)
  local copies, waits for them, and re-layouts  110 us (13%)
  matrix products  82.2 us (10%)
  blocking collectives  71.8 us (8%)
  other arithmetic  66.4 us (8%)
  between operations  16.1 us (2%)
  starting transfers between devices  15.7 us (2%)
    unnamed x14, waiting for transfers between devices  203 us
    reduce_scatter x1, waiting for transfers between devices, on_device(): lax.psum_scatter(g_down * grad_scale, 'dp', scatter_dimension=1, tiled=True)  69.6 us
    psum x1, waiting for transfers between devices, on_device(): attended = lax.psum(attn_part, 'tensor')  58.2 us
    psum x1, waiting for transfers between devices, on_device(): lax.psum(d_normed_part.astype(jnp.bfloat16), 'tensor').astype(jnp.float32)  54.8 us
    psum x1, blocking collectives, on_device(): lax.psum((g_qv_bias * grad_scale, g_up_bias * grad_scale), 'dp')  44.6 us
    psum x1, waiting for transfers between devices, on_device(): lax.psum(ffn_part.astype(jnp.bfloat16), 'tensor').astype(jnp.float32)  43.8 us
    unnamed x135, local copies, waits for them, and re-layouts  31.6 us
    all_to_all x1, blocking collectives, on_device(): lax.all_to_all(tokens, 'dp', split_axis=0, concat_axis=0, tiled=True)  27.3 us
  transfers between devices with their start and end apart: 13, of which 10 were waited for; matrix products, arithmetic and copies ran while one was open for 14% of the time, Pallas kernels for 0%

commit v1 on v0

--- a/solution.py
+++ b/solution.py
@@ -99,7 +99,12 @@
     )
     context = context.reshape(row_count, local_heads * HEAD_DIM).astype(jnp.bfloat16)
     attn_part = jnp.dot(context, out_weight, preferred_element_type=jnp.float32)
-    attended = lax.psum(attn_part, "tensor")
+    wide_n = lax.axis_size("tensor")
+    attended = attn_part
+    for i0 in [
+        [(c, c ^ tick) for c in range(wide_n)] for tick in (1, 2, 4, 8, 16) if tick < wide_n
+    ]:
+        attended = attended + lax.ppermute(attended, "tensor", i0)
     hidden = packed_in.astype(jnp.float32) + (attended + out_bias.astype(jnp.float32))
     normed, first_pull = jax.vjp(
         layer_norm, hidden, first_gain.astype(jnp.float32), first_shift.astype(jnp.float32)

time: 856 us -> 889 us (1.039)
  waiting for transfers between devices: 487 us -> 507 us
  local copies, waits for them, and re-layouts: 110 us -> 121 us
    ppermute x0 -> x2, waiting for transfers between devices: none -> 84.2 us  [on_device(): attended = attended + lax.ppermute(attended, 'tensor', i0)]
    psum x1 -> x0, waiting for transfers between devices: 58.2 us -> none  [on_device(): attended = lax.psum(attn_part, 'tensor')]
    unnamed x135 -> x130, local copies, waits for them, and re-layouts: 31.6 us -> 33.7 us
    unnamed x14 -> x12, waiting for transfers between devices: 203 us -> 204 us
  transfers between devices with their start and end apart: 13 -> 14, of which waited for: 10 -> 10; matrix products, arithmetic and copies ran while one was open for 14% -> 15% of each run, Pallas kernels for 0% -> 0%
where the time goes in v1:
time: 889 us; the launch traced here: 882 us
  waiting for transfers between devices  507 us (57%)
  local copies, waits for them, and re-layouts  121 us (14%)
  blocking collectives  74.9 us (8%)
  matrix products  73.8 us (8%)
  other arithmetic  72.8 us (8%)
  starting transfers between devices  16.7 us (2%)
  between operations  15.9 us (2%)
    unnamed x12, waiting for transfers between devices  204 us
    ppermute x2, waiting for transfers between devices, on_device(): attended = attended + lax.ppermute(attended, 'tensor', i0)  84.2 us
    reduce_scatter x1, waiting for transfers between devices, on_device(): lax.psum_scatter(g_down * grad_scale, 'dp', scatter_dimension=1, tiled=True)  69.6 us
    psum x1, waiting for transfers between devices, on_device(): lax.psum(d_normed_part.astype(jnp.bfloat16), 'tensor').astype(jnp.float32)  55.8 us
    psum x1, blocking collectives, on_device(): lax.psum((g_qv_bias * grad_scale, g_up_bias * grad_scale), 'dp')  47.6 us
    psum x1, waiting for transfers between devices, on_device(): lax.psum(ffn_part.astype(jnp.bfloat16), 'tensor').astype(jnp.float32)  36.8 us
    unnamed x130, local copies, waits for them, and re-layouts  33.7 us
    all_to_all x1, blocking collectives, on_device(): lax.all_to_all(tokens, 'dp', split_axis=0, concat_axis=0, tiled=True)  27.3 us
  transfers between devices with their start and end apart: 14, of which 10 were waited for; matrix products, arithmetic and copies ran while one was open for 15% of the time, Pallas kernels for 0%

profile of v1, /device:TPU:0, one launch (start us, length us, event | category | flops | bytes accessed | tf_op | source)
XLA Modules:
  0.0 881.7 jit_solution(14229800986557239957)
XLA Ops:
  7.3 1.9 all_to_all.28
  9.3 27.3 %all_to_all.42 = bf16[8,192,192]{1,2,0:T(8,128)(2,1)S(1)} all-to-all(bf16[8,192,192]{1,2,0:T(8,128)(2,1)S(1)} %copy.118), channel_id=1, replica_groups=mesh['dp'=8,'tensor'=4] {'dp'}, dimensions={0} | all-to-all | bytes 1179648 | tf_op jit(solution)/shard_map/all_to_all | solution.py:63
  40.4 2.1 broadcast_multiply_fusion
  42.5 19.3 %all-gather.3.cloned.1.call-done = bf16[1536,768]{0,1:T(8,128)(2,1)} async-done(((bf16[1536,192]{0,1:T(8,128)(2,1)}), bf16[1536,768]{0,1:T(8,128)(2,1)}) %all-gather.3.cloned.1.call-update) | async-done | bytes 2359312 | tf_op jit(solution)/shard_map/all_gather | solution.py:67
  61.7 4.3 copy.120
  66.0 9.8 %scatter_custom_fusion = bf16[1536,768]{1,0:T(8,128)(2,1)} fusion(s32[1536]{0:T(1024)S(1)} %fusion.70, bf16[1536,768]{1,0:T(8,128)(2,1)} %copy.120, bf16[]{:T(256)} %constant.46.clone.1), kind=kCustom, calls=%fused_computation.107 | custom fusion | bytes 2359808 | tf_op jit(solution)/shard_map/scatter | solution.py:71
  75.8 3.2 fusion.85
  84.0 5.3 fusion.84
  90.7 2.4 copy-done.2
  93.0 1.9 fusion.45
  96.8 7.7 collective-permute-done
  104.5 3.2 add.182
  108.0 2.4 all_to_all.33
  110.4 2.2 copy.131
  112.6 5.7 all-to-all-start.2
  118.7 20.1 %all-to-all-done.2 = bf16[8,192,192]{1,2,0:T(8,128)(2,1)} async-done(((bf16[8,192,192]{1,2,0:T(8,128)(2,1)}), bf16[8,192,192]{1,2,0:T(8,128)(2,1)}, u32[]{:S(2)}, u32[]{:S(2)}) %all-to-all-start.2) | async-done | bytes 589856 | tf_op jit(solution)/shard_map/all_to_all | solution.py:64
  138.8 2.5 copy.132
  141.2 2.5 all_to_all.35
  143.8 4.3 copy.121
  148.0 76.5 %collective-permute-done.1 = f32[1536,768]{0,1:T(8,128)} collective-permute-done((f32[1536,768]{0,1:T(8,128)}, f32[1536,768]{0,1:T(8,128)}, u32[]{:S(2)}, u32[]{:S(2)}) %collective-permute-start.1) | collective-permute-done | bytes 4718624 | tf_op jit(solution)/shard_map/ppermute | solution.py:107
  224.6 5.3 fusion.81
  230.4 4.5 add_bitcast_fusion
  235.0 11.5 %multiply_convert_fusion.2 = (bf16[1536,768]{1,0:T(8,128)(2,1)S(1)}, f32[1536,768]{1,0:T(8,128)}) fusion(f32[2,1536,768]{2,1,0:T(8,128)S(1)} %add_bitcast_fusion), kind=kLoop, calls=%fused_computation.51 | loop fusion | flops 77856768 | bytes 16515072 | tf_op jit(solution)/shard_map/convert_element_type | solution.py:116
  247.9 3.5 convolution_convert_fusion
  252.0 4.3 copy.133
  256.3 9.8 %scatter_custom_fusion.1 = bf16[1536,768]{1,0:T(8,128)(2,1)} fusion(s32[1536]{0:T(1024)} %copy-done.27, bf16[1536,768]{1,0:T(8,128)(2,1)} %copy.133, bf16[]{:T(256)} %constant.46.clone.1), kind=kCustom, calls=%fused_computation.105 | custom fusion | bytes 2359808 | tf_op jit(solution)/shard_map/scatter | solution.py:72
  266.1 4.3 copy.134
  270.4 36.8 %all-reduce.12.cloned.1.call-done = bf16[1536,768]{0,1:T(8,128)(2,1)} async-done(((bf16[1536,768]{0,1:T(8,128)(2,1)}), bf16[1536,768]{0,1:T(8,128)(2,1)}) %all-reduce.12.cloned.1.call-update) | async-done | bytes 2359312 | tf_op jit(solution)/shard_map/psum | solution.py:118
  307.3 4.0 fusion.79
  311.3 2.2 fusion.4
  313.5 4.4 fusion.78
  317.9 2.2 fusion.58
  322.4 2.6 fusion.35
  327.1 5.1 bitcast_convert_fusion.1
  332.3 55.8 %all-reduce.14.cloned.1.call-done = bf16[1536,768]{0,1:T(8,128)(2,1)} async-done(((bf16[1536,768]{0,1:T(8,128)(2,1)}), bf16[1536,768]{0,1:T(8,128)(2,1)}) %all-reduce.14.cloned.1.call-update) | async-done | bytes 2359312 | tf_op jit(solution)/shard_map/psum | solution.py:136
  388.1 6.2 fusion.76
  394.4 4.3 multiply_reduce_fusion.1
  398.7 4.4 fusion.77
  403.0 2.2 copy-done.5
  406.4 5.3 fusion.46
  411.7 7.2 multiply_reduce_fusion
  418.9 11.2 %multiply_convert_fusion = bf16[3,3,512,512]{2,3,1,0:T(8,128)(2,1)} fusion(f32[3,3,512,512]{2,3,1,0:T(8,128)} %get-tuple-element.113, f32[3,3,512,512]{2,3,1,0:T(8,128)} %copy-done.2, f32[3,3,512]{2,1,0:T(4,128)S(1)} %get-tuple-element.112, f32[3,3,512]{2,1,0:T(4,128)S(1)} %log_add_fusion), kind=kLoop, calls=%fused_computation.5 | loop fusion | flops 9437184 | bytes 23629824 | tf_op jit(solution)/shard_map/convert_element_type | solution.py:158
  430.1 4.0 fusion.49
  437.4 2.7 copy.140
  440.1 1.8 stack.34
  443.4 1.8 stack.35
  446.6 4.6 bitcast_convert_fusion
  451.3 3.4 convolution_multiply_fusion.3
  456.0 10.4 %multiply_bitcast_fusion = f32[2,768,768]{1,2,0:T(8,128)} fusion(bf16[1,1536,768]{2,1,0:T(8,128)(2,1)} %copy-done.11, bf16[1,1536,768]{2,1,0:T(8,128)(2,1)S(1)} %copy-done.10, f32[1536,768]{0,1:T(8,128)} %copy-done.3, f32[768]{0:T(1024)} %copy-done.30, f32[768]{0:T(1024)} %copy-done.24, f32[1536]{0:T(1024)S(1)} %fusion.68, ...), kind=kOutput, calls=%fused_computation.43 | convolution fusion | flops 3633315840 | bytes 14174208 | tf_op jit(solution)/shard_map/td,ktf->kdf/dot_general | solution.py:131
  466.4 8.3 copy.151
  476.4 4.3 multiply_bitcast_fusion.1
  480.6 4.2 copy.168
  484.9 4.8 reshape.282
  490.1 5.8 convolution_multiply_fusion
  497.8 5.4 gather_fusion
  503.2 5.4 all-to-all-start.1
  509.9 3.1 convert_reduce_fusion
  513.0 16.8 %all-to-all-done.1 = bf16[8,192,192]{2,1,0:T(8,128)(2,1)S(1)} async-done(((bf16[8,192,192]{2,1,0:T(8,128)(2,1)}), bf16[8,192,192]{2,1,0:T(8,128)(2,1)S(1)}, u32[]{:S(2)}, u32[]{:S(2)}) %all-to-all-start.1) | async-done | bytes 589856 | tf_op jit(solution)/shard_map/all_to_all | solution.py:207
  532.8 5.4 gather_fusion.1
  538.1 3.6 all-to-all-start.3
  543.4 47.6 %all-reduce.7 = (f32[2,192]{1,0:T(2,128)}, f32[768]{0:T(1024)S(1)}, f32[768]{0:T(1024)S(1)}, f32[768]{0:T(1024)S(1)}, f32[2,768]{1,0:T(2,128)}, /*index=5*/f32[7...) all-reduce(f32[2,192]{1,0:T(2,128)S(1)} %broadcast_multiply_fusion.10, ...), channel_id=1, replica_groups=mesh['dp'=8,'tensor'=4] {'dp'}, use_global_device_ids=true, to_apply=%region_18.19 | all-reduce | flops 6528 | bytes 52224 | tf_op jit(solution)/shard_map/psum | solution.py:202
  596.1 136.0 %all-reduce.16.cloned.1.call-done = f32[2,768,768]{2,0,1:T(2,128)} async-done(((f32[2,768,768]{2,0,1:T(2,128)}), f32[2,768,768]{2,0,1:T(2,128)}) %all-reduce.16.cloned.1.call-update) | async-done | bytes 4718608
  734.0 68.0 %reduce-scatter.13.cloned.1.call-done = f32[96,576]{1,0:T(8,128)} async-done(((f32[768,576]{1,0:T(8,128)}), f32[96,576]{1,0:T(8,128)}) %reduce-scatter.13.cloned.1.call-update) | async-done | bytes 221200
  805.0 69.6 %reduce-scatter.11.cloned.1.call-done = f32[768,96]{0,1:T(8,128)} async-done(((f32[768,768]{0,1:T(8,128)}), f32[768,96]{0,1:T(8,128)}) %reduce-scatter.11.cloned.1.call-update) | async-done | bytes 294928 | tf_op jit(solution)/shard_map/reduce_scatter | solution.py:183
  (210 shorter events, 47.2 us)
Async XLA Ops:
  7.2 223.3 %copy-start = (bf16[2,768,768]{2,1,0:T(8,128)(2,1)S(1)}, bf16[2,768,768]{2,1,0:T(8,128)(2,1)}, u32[]{:S(2)}) copy-start(bf16[2,768,768]{2,1,0:T(8,128)(2,1)} %param.26) | copy-start | bytes 7077892
  7.2 31.4 %copy-start.36 = (s32[1536]{0:T(1024)S(1)}, s32[1536]{0:T(1024)}, u32[]{:S(2)}) copy-start(s32[1536]{0:T(1024)} %param.18) | copy-start | bytes 18436
  7.2 31.5 %copy-start.37 = (s32[1,1536]{1,0:T(1,128)S(1)}, s32[1,1536]{1,0:T(1,128)}, u32[]{:S(2)}) copy-start(s32[1,1536]{1,0:T(1,128)} %param.19) | copy-start | bytes 18436
  7.2 31.5 %copy-start.40 = (bf16[2,192]{1,0:T(2,128)(2,1)S(1)}, bf16[2,192]{1,0:T(2,128)(2,1)}, u32[]{:S(2)}) copy-start(bf16[2,192]{1,0:T(2,128)(2,1)} %param.21) | copy-start | bytes 2308
  7.2 54.5 %all-gather.3.cloned.1.call-start = ((), (), s32[]{:S(2)}) async-start(), calls=%async_computation.8 | async-start | bytes 2949120 | tf_op jit(solution)/shard_map/all_gather | solution.py:67
  38.7 27.3 %copy-start.27 = (s32[1536]{0:T(1024)}, s32[1536]{0:T(1024)S(1)}, u32[]{:S(2)}) copy-start(s32[1536]{0:T(1024)S(1)} %fusion.70) | copy-start | bytes 18436
  40.3 35.5 %copy-start.49 = (bf16[3,768,192]{1,2,0:T(8,128)(2,1)S(1)}, bf16[3,768,192]{1,2,0:T(8,128)(2,1)}, u32[]{:S(2)}) copy-start(bf16[3,768,192]{1,2,0:T(8,128)(2,1)} %param.20) | copy-start | bytes 2654212
  84.0 5.3 copy-start.13
  89.3 3.7 copy-start.2
  89.3 3.7 copy-start.18
  93.0 2.6 copy-start.22
  96.5 22.1 %copy-start.42 = (bf16[768]{0:T(1024)(128)(2,1)S(1)}, bf16[768]{0:T(1024)(128)(2,1)}, u32[]{:S(2)}) copy-start(bf16[768]{0:T(1024)(128)(2,1)} %param.24) | copy-start | bytes 4612
  96.5 22.2 %copy-start.43 = (bf16[768]{0:T(1024)(128)(2,1)S(1)}, bf16[768]{0:T(1024)(128)(2,1)}, u32[]{:S(2)}) copy-start(bf16[768]{0:T(1024)(128)(2,1)} %param.25) | copy-start | bytes 4612
  96.5 22.2 %copy-start.44 = (bf16[768]{0:T(1024)(128)(2,1)S(1)}, bf16[768]{0:T(1024)(128)(2,1)}, u32[]{:S(2)}) copy-start(bf16[768]{0:T(1024)(128)(2,1)} %param.23) | copy-start | bytes 4612
  96.5 22.2 %copy-start.41 = (bf16[2,768]{1,0:T(2,128)(2,1)S(1)}, bf16[2,768]{1,0:T(2,128)(2,1)}, u32[]{:S(2)}) copy-start(bf16[2,768]{1,0:T(2,128)(2,1)} %param.27) | copy-start | bytes 9220
  96.5 8.0 collective-permute-start
  107.7 116.9 %collective-permute-start.1 = (f32[1536,768]{0,1:T(8,128)}, f32[1536,768]{0,1:T(8,128)}, u32[]{:S(2)}, u32[]{:S(2)}) collective-permute-start(f32[1536,768]{0,1:T(8,128)} %add.182), channel_id=1, source_target_pairs={{0,2},{1,3},{2,0},{3,1},{4,6},{5,7},{6,4},{7,5},{8,10},{9,11},{10,... | collective-permute-start | bytes 14155784 | tf_op jit(solution)/shard_map/ppermute | solution.py:107
  112.6 26.1 %all-to-all-start.2 = ((bf16[8,192,192]{1,2,0:T(8,128)(2,1)}), bf16[8,192,192]{1,2,0:T(8,128)(2,1)}, u32[]{:S(2)}, u32[]{:S(2)}) async-start(bf16[8,192,192]{1,2,0:T(8,128)(2,1)} %copy.131), calls=%async_computation.2 | async-start | bytes 1572864 | tf_op jit(solution)/shard_map/all_to_all | solution.py:64
  118.3 133.7 %all-gather.5.cloned.1.call-start = ((), (), s32[]{:S(2)}) async-start(), calls=%async_computation.10 | async-start | bytes 2949120 | tf_op jit(solution)/shard_map/all_gather | solution.py:68
  118.6 280.1 %copy-start.24 = (f32[768]{0:T(1024)}, f32[768]{0:T(1024)S(1)}, u32[]{:S(2)}) copy-start(f32[768]{0:T(1024)S(1)} %convert_element_type.142) | copy-start | bytes 9220
  118.7 188.6 %copy-start.30 = (f32[768]{0:T(1024)}, f32[768]{0:T(1024)S(1)}, u32[]{:S(2)}) copy-start(f32[768]{0:T(1024)S(1)} %convert_element_type.143) | copy-start | bytes 9220
  143.7 163.6 %all-reduce.12.cloned.1.call-start = ((), (), s32[]{:S(2)}) async-start(), calls=%async_computation.9 | async-start | bytes 4718592 | tf_op jit(solution)/shard_map/psum | solution.py:118
  229.9 5.1 copy-start.3
  234.9 11.5 %copy-start.6 = (f32[2,1536,768]{2,1,0:T(8,128)}, f32[2,1536,768]{2,1,0:T(8,128)S(1)}, u32[]{:S(2)}) copy-start(f32[2,1536,768]{2,1,0:T(8,128)S(1)} %add_bitcast_fusion) | copy-start | bytes 28311556
  234.9 13.0 %copy-start.47 = (bf16[768,768]{1,0:T(8,128)(2,1)S(1)}, bf16[768,768]{1,0:T(8,128)(2,1)}, u32[]{:S(2)}) copy-start(bf16[768,768]{1,0:T(8,128)(2,1)} %param.28) | copy-start | bytes 3538948
  247.9 4.0 copy-start.38
  247.9 4.0 copy-start.45
  251.5 136.7 %all-reduce.14.cloned.1.call-start = ((), (), s32[]{:S(2)}) async-start(), calls=%async_computation.11 | async-start | bytes 4718592 | tf_op jit(solution)/shard_map/psum | solution.py:136
  307.3 4.0 copy-start.7
  313.5 4.4 copy-start.48
  313.5 6.8 slice-start
  313.5 6.8 slice-start.1
  313.5 8.4 slice-start.3
  317.9 2.4 copy-start.8
  317.9 70.2 %copy-start.25 = (f32[1536]{0:T(1024)}, f32[1536]{0:T(1024)S(1)}, u32[]{:S(2)}) copy-start(f32[1536]{0:T(1024)S(1)} %negate_multiply_fusion.2) | copy-start | bytes 18436
  317.9 4.4 slice-start.2
  317.9 4.5 slice-start.4
  332.2 198.6 %reduce-scatter.9.cloned.1.call-start = ((), (), s32[]{:S(2)}) async-start(), calls=%async_computation.12 | async-start | bytes 2949120 | tf_op jit(solution)/shard_map/reduce_scatter | solution.py:173
  406.4 5.3 copy-start.19
  418.9 11.2 %copy-start.14 = (bf16[3,512,3,64]{1,0,3,2:T(4,128)(2,1)S(1)}, bf16[3,512,3,64]{1,0,3,2:T(4,128)(2,1)}, u32[]{:S(2)}) copy-start(bf16[3,512,3,64]{1,0,3,2:T(4,128)(2,1)} %copy-done.13) | copy-start | bytes 1769476
  430.1 4.0 copy-start.4
  430.1 4.0 copy-start.17
  437.4 13.8 %copy-start.15 = (bf16[1,1536,192]{1,2,0:T(8,128)(2,1)}, bf16[1,1536,192]{1,2,0:T(8,128)(2,1)S(1)}, u32[]{:S(2)}) copy-start(bf16[1,1536,192]{1,2,0:T(8,128)(2,1)S(1)} %stack.36) | copy-start | bytes 1769476
  441.9 9.3 %copy-start.16 = (bf16[1,1536,192]{1,2,0:T(8,128)(2,1)}, bf16[1,1536,192]{1,2,0:T(8,128)(2,1)S(1)}, u32[]{:S(2)}) copy-start(bf16[1,1536,192]{1,2,0:T(8,128)(2,1)S(1)} %stack.34) | copy-start | bytes 1769476
  451.2 4.8 copy-start.10
  451.2 143.2 %reduce-scatter.15.cloned.1.call-start = ((), (), s32[]{:S(2)}) async-start(), calls=%async_computation.15 | async-start | bytes 884736
  455.9 276.1 %all-reduce.16.cloned.1.call-start = ((), (), s32[]{:S(2)}) async-start(), calls=%async_computation.16 | async-start | bytes 9437184
  474.7 327.4 %reduce-scatter.13.cloned.1.call-start = ((), (), s32[]{:S(2)}) async-start(), calls=%async_computation.14 | async-start | bytes 2211840
  484.9 5.2 copy-start.21
  484.9 5.2 copy-start.26
  489.7 6.2 copy-start.39
  489.7 6.2 copy-start.46
  489.7 6.3 copy-start.28
  489.8 384.9 %reduce-scatter.11.cloned.1.call-start = ((), (), s32[]{:S(2)}) async-start(), calls=%async_computation.13 | async-start | bytes 2654208 | tf_op jit(solution)/shard_map/reduce_scatter | solution.py:183
  497.5 11.1 %copy-start.50 = (u32[32]{0:T(128)S(1)}, u32[32]{0:T(128)}, u32[]{:S(2)}) copy-start(u32[32]{0:T(128)} %constant.120) | copy-start | bytes 388
  497.5 12.3 %copy-start.31 = (f32[768]{0:T(1024)S(1)}, f32[768]{0:T(1024)}, u32[]{:S(2)}) copy-start(f32[768]{0:T(1024)} %get-tuple-element.100) | copy-start | bytes 9220
  503.2 26.6 %all-to-all-start.1 = ((bf16[8,192,192]{2,1,0:T(8,128)(2,1)}), bf16[8,192,192]{2,1,0:T(8,128)(2,1)S(1)}, u32[]{:S(2)}, u32[]{:S(2)}) async-start(bf16[8,192,192]{2,1,0:T(8,128)(2,1)} %bitcast.11), calls=%async_computation.1 | async-start | bytes 1572864 | tf_op jit(solution)/shard_map/all_to_all | solution.py:207
  532.7 10.6 %copy-start.32 = (f32[768]{0:T(1024)S(1)}, f32[768]{0:T(1024)}, u32[]{:S(2)}) copy-start(f32[768]{0:T(1024)} %get-tuple-element.87) | copy-start | bytes 9220
  532.7 10.6 %copy-start.33 = (f32[768]{0:T(1024)S(1)}, f32[768]{0:T(1024)}, u32[]{:S(2)}) copy-start(f32[768]{0:T(1024)} %get-tuple-element.74) | copy-start | bytes 9220
  532.7 10.6 %copy-start.34 = (f32[768]{0:T(1024)S(1)}, f32[768]{0:T(1024)}, u32[]{:S(2)}) copy-start(f32[768]{0:T(1024)} %get-tuple-element.102) | copy-start | bytes 9220
  532.7 10.6 %copy-start.29 = (f32[768]{0:T(1024)S(1)}, f32[768]{0:T(1024)}, u32[]{:S(2)}) copy-start(f32[768]{0:T(1024)} %get-tuple-element.76) | copy-start | bytes 9220
  532.8 10.6 %copy-start.35 = (f32[768]{0:T(1024)S(1)}, f32[768]{0:T(1024)}, u32[]{:S(2)}) copy-start(f32[768]{0:T(1024)} %get-tuple-element.70) | copy-start | bytes 9220
  532.8 341.9 %copy-start.1 = (bf16[2,768,768]{2,1,0:T(8,128)(2,1)S(1)}, bf16[2,768,768]{2,1,0:T(8,128)(2,1)}, u32[]{:S(2)}) copy-start(bf16[2,768,768]{2,1,0:T(8,128)(2,1)} %param.26) | copy-start | bytes 7077892
  538.1 265.8 %all-to-all-start.3 = ((bf16[8,192,192]{2,1,0:T(8,128)(2,1)}), bf16[8,192,192]{2,1,0:T(8,128)(2,1)S(1)}, u32[]{:S(2)}, u32[]{:S(2)}) async-start(bf16[8,192,192]{2,1,0:T(8,128)(2,1)} %bitcast.196), calls=%async_computation.4 | async-start | bytes 1572864 | tf_op jit(solution)/shard_map/all_to_all | solution.py:208
  (6 other events, 10.1 us)
Sparse Core Ops, SparseCore 0:
  38.7 23.0 all-gather.2
  143.8 35.7 all-gather.4
  251.6 55.6 all-reduce.11
  332.4 55.7 all-reduce.13
  451.3 32.8 reduce-scatter.8
  487.4 68.3 reduce-scatter.14
  559.4 172.6 all-reduce.15
  735.5 66.4 reduce-scatter.12
  806.2 68.4 reduce-scatter.10
